TPU v7x, 512 devices: a whole 4x4x16 slice. The times are simulated.
512 devices in a mesh: grp: 32 (over x, y, z_hi), tile: 16 (over z_lo, core).
Axes of the slice: x: 4, y: 4, z: 16 (z_hi: 2, z_lo: 8; z = z_hi * 8 + z_lo), core: 2. Of those that a mesh axis runs over, the one named last changes fastest.
Arguments:
- log_cond: float32 [32, 128, 32, 128], P('grp', 'tile'), may hold values from -3 to 3
- potential: float32 [32, 128, 32, 128], P('grp', 'tile'), may hold values from -6 to 6
- noise: float32 [2, 32, 128, 32, 128], P(None, 'grp', 'tile'), may hold values from -3 to 3
- source: float32 [128, 32, 128], P('tile'), may hold values from -6 to 6
- parents: int32 [32], replicated, may hold values from 0 to 31
- accept: int32 [2, 32], P(None, 'grp'), may hold values 0 or 1
- weights: float32 [32], P('grp'), may hold values from 0.1 to 10
Outputs:
- conduct_out: float32 [32, 128, 32, 128], P('grp', 'tile')
- potential_out: float32 [32, 128, 32, 128], P('grp', 'tile')
- moments: float32 [1024, 1024], P('tile')
Inputs may be any that keep to these rules, and one draw needn't show every extreme that they name: `parents`: parent indices of offspring.
All inputs are finite; a program needn't handle non-finite values. No bound on the sum of `accept` on one device may be relied on, other than what follows from the above.
Results may differ from a plain program's by a relative error of at most 0.0001.
Values sent between devices are 32-bit elements; how exact they have to be, the bound alone decides.
A program may use at most 64 MiB of HBM per device.

v0:
```python
import jax
import jax.numpy as jnp
from jax import lax
from jax.sharding import PartitionSpec as P

prior_keep = 0.8
prior_fresh = 0.6
relax_weight = 0.8


def with_halo(block, sides, width):
    for axis, dim in sides:
        count = lax.axis_size(axis)
        forward = [(i, i + 1) for i in range(count - 1)]
        backward = [(target, source) for source, target in forward]
        low = lax.ppermute(
            lax.slice_in_dim(block, block.shape[dim] - width, None, axis=dim), axis, forward
        )
        high = lax.ppermute(lax.slice_in_dim(block, 0, width, axis=dim), axis, backward)
        block = jnp.concatenate([low, block, high], axis=dim)
    return block


def neighbours(padded):
    return [
        padded[2:, 1:-1, 1:-1],
        padded[:-2, 1:-1, 1:-1],
        padded[1:-1, 2:, 1:-1],
        padded[1:-1, :-2, 1:-1],
        padded[1:-1, 1:-1, 2:],
        padded[1:-1, 1:-1, :-2],
    ]


def relax_sweep(cond_ext, pot_ext, source):
    cond_pad = jnp.pad(cond_ext, ((0, 0), (1, 1), (1, 1)))
    pot_pad = jnp.pad(pot_ext, ((0, 0), (1, 1), (1, 1)))
    conductivity = jnp.exp(cond_pad)
    centre_k = conductivity[1:-1, 1:-1, 1:-1]
    centre = pot_pad[1:-1, 1:-1, 1:-1]
    flux_sum = jnp.zeros_like(centre)
    coef_sum = jnp.zeros_like(centre)
    for near_k, near_v in zip(neighbours(conductivity), neighbours(pot_pad)):
        face = 0.5 * (centre_k + near_k)
        flux_sum = flux_sum + face * near_v
        coef_sum = coef_sum + face
    return (1.0 - relax_weight) * centre + relax_weight * (source + flux_sum) / coef_sum


def local(log_cond, potential, noise, source, parents, accept, weights):
    mine = lax.axis_index("grp")
    bundle = jnp.stack([log_cond[0], potential[0]])
    parent = parents[mine]
    pieces = lax.all_gather(bundle[None], "grp", axis=0, tiled=True)
    owners = jnp.arange(pieces.shape[0], dtype=jnp.int32)
    chosen = jnp.where((owners == parent)[:, None, None, None, None], pieces, 0.0)
    moved = jnp.sum(chosen, axis=0)
    conduct = moved[0]
    pot = moved[1]
    width = conduct.shape[0]
    for move_index in range(noise.shape[0]):
        proposal = prior_keep * conduct + prior_fresh * noise[move_index, 0]
        extended = with_halo(jnp.stack([proposal, pot]), (("tile", 1),), 1)
        relaxed_once = relax_sweep(extended[0], extended[1], source)
        pot_ext = with_halo(relaxed_once, (("tile", 0),), 1)
        relaxed_twice = relax_sweep(extended[0], pot_ext, source)
        accepted = accept[move_index, 0] > 0
        conduct = jnp.where(accepted, proposal, conduct)
        pot = jnp.where(accepted, relaxed_twice, pot)
    weight_sum = lax.psum(jnp.sum(weights), "grp")
    share = weights[0] / weight_sum
    traces = jnp.transpose(pot, (1, 0, 2)).reshape(pot.shape[1], width * pot.shape[2])
    product = lax.dot_general(
        traces,
        traces,
        (((0,), (0,)), ((), ())),
        precision=lax.Precision.HIGHEST,
        preferred_element_type=jnp.float32,
    )
    partial_rows = lax.psum_scatter(share * product, "tile", scatter_dimension=0, tiled=True)
    moments = lax.psum(partial_rows, "grp")
    return (conduct[None], pot[None], moments)


def solution(mesh):
    placed = (
        P("grp", "tile", None, None),
        P("grp", "tile", None, None),
        P(None, "grp", "tile", None, None),
        P("tile", None, None),
        P(),
        P(None, "grp"),
        P("grp"),
    )
    return jax.shard_map(
        local,
        mesh=mesh,
        in_specs=placed,
        out_specs=(P("grp", "tile", None, None), P("grp", "tile", None, None), P("tile", None)),
        check_vma=False,
    )
```

profile of v0, /device:TPU:14, one launch (start us, length us, event | category | flops | bytes accessed | tf_op | source)
XLA Modules:
  0.0 1160.8 jit_solution(12140395760338257270)
XLA Ops:
  7.2 0.0 all-gather.3.cloned.1.call-start
  7.2 1.7 pad_maximum_fusion.2
  8.9 0.0 all-gather.3.cloned.1.call-update
  8.9 0.0 reduce-scatter.2.cloned.1.call-start
  9.0 1.3 fusion.101
  11.6 1.2 dynamic_slice.3
  12.8 0.6 iota_compare_fusion.4
  13.5 247.6 %all-gather.3.cloned.1.call-done = f32[64,8,32,128]{3,2,1,0:T(8,128)} async-done(((f32[2,8,32,128]{3,2,1,0:T(8,128)}), f32[64,8,32,128]{3,2,1,0:T(8,128)}) %all-gather.3.cloned.1.call-update) | async-done | bytes 8388624 | tf_op jit(solution)/shard_map/all_gather | solution.py:54
  261.1 0.0 copy-start.2
  261.1 0.0 copy-start
  261.1 4.6 select_reduce_fusion
  265.8 0.0 copy-done.2
  265.8 0.7 broadcast_select_fusion
  266.5 1.3 collective-permute-start
  267.8 1.3 collective-permute-start.1
  269.1 0.0 collective-permute-done
  269.1 1.8 collective-permute-done.1
  271.0 0.0 copy-done
  271.0 0.3 fusion.11
  271.3 1.3 collective-permute-start.2
  272.6 3.0 collective-permute-start.3
  275.6 0.0 collective-permute-done.2
  275.6 0.8 collective-permute-done.3
  276.4 0.2 select_maximum_fusion.2
  276.6 0.3 fusion.85
  276.9 7.9 collective-permute-start.4
  284.9 1.3 collective-permute-start.5
  286.2 0.0 collective-permute-done.4
  286.2 3.9 collective-permute-done.5
  290.1 0.3 fusion.23
  290.4 1.3 collective-permute-start.6
  291.7 6.7 collective-permute-start.7
  298.4 137.9 %psum.14 = f32[]{:T(128)} all-reduce(f32[]{:T(128)} %bitcast.17), channel_id=1, replica_groups=mesh['grp'=32,'tile'=16] {'grp'}, use_global_device_ids=true, to_apply=%region_1.2 | all-reduce | flops 1 | bytes 8 | tf_op jit(solution)/shard_map/psum | solution.py:70
  437.7 0.0 collective-permute-done.6
  437.7 0.0 collective-permute-done.7
  437.7 0.2 select_maximum_fusion
  437.9 0.3 fusion.66
  438.2 0.0 copy-start.1
  438.2 5.1 convolution_multiply_fusion
  443.3 0.0 reduce-scatter.2.cloned.1.call-update
  443.3 0.0 copy-done.1
  443.3 0.0 all-reduce.8.cloned.1.call-start
  443.3 130.4 %reduce-scatter.2.cloned.1.call-done = f32[64,1024]{1,0:T(8,128)} async-done(((f32[1024,1024]{1,0:T(8,128)}), f32[64,1024]{1,0:T(8,128)}) %reduce-scatter.2.cloned.1.call-update) | async-done | bytes 262160 | tf_op jit(solution)/shard_map/reduce_scatter | solution.py:80
  573.8 0.0 all-reduce.8.cloned.1.call-update
  573.8 578.8 %all-reduce.8.cloned.1.call-done = f32[64,1024]{1,0:T(8,128)} async-done(((f32[64,1024]{1,0:T(8,128)}), f32[64,1024]{1,0:T(8,128)}) %all-reduce.8.cloned.1.call-update) | async-done | bytes 262160 | tf_op jit(solution)/shard_map/psum | solution.py:81
  1152.6 1.7 copy.19
  (8 shorter events, 0.1 us)
Async XLA Ops:
  7.2 254.0 %all-gather.3.cloned.1.call-start = ((), (), s32[]{:S(2)}) async-start(), calls=%async_computation.3 | async-start | bytes 8650752 | tf_op jit(solution)/shard_map/all_gather | solution.py:54
  8.9 564.9 %reduce-scatter.2.cloned.1.call-start = ((), (), s32[]{:S(2)}) async-start(), calls=%async_computation.1 | async-start | bytes 4456448 | tf_op jit(solution)/shard_map/reduce_scatter | solution.py:80
  261.1 4.6 copy-start.2
  261.1 9.8 copy-start
  266.5 2.6 collective-permute-start
  267.8 3.1 collective-permute-start.1
  271.3 4.3 collective-permute-start.2
  272.6 3.9 collective-permute-start.3
  276.9 9.2 collective-permute-start.4
  284.9 5.2 collective-permute-start.5
  290.4 147.2 %collective-permute-start.6 = (f32[1,32,128]{2,1,0:T(8,128)S(1)}, f32[1,32,128]{2,1,0:T(8,128)S(1)}, u32[]{:S(2)}, u32[]{:S(2)}) collective-permute-start(f32[1,32,128]{2,1,0:T(8,128)S(1)} %get-tuple-element.16), channel_id=1, source_target_pairs={{1,0},{2,1},{3,2},{4,3},{5,4},{6,5},{7,6},{8,7},{9,8},{10,9},{11,1... | collective-permute-start | bytes 49160 | tf_op jit(solution)/shard_map/ppermute | solution.py:19
  291.7 146.0 %collective-permute-start.7 = (f32[1,32,128]{2,1,0:T(8,128)S(1)}, f32[1,32,128]{2,1,0:T(8,128)S(1)}, u32[]{:S(2)}, u32[]{:S(2)}) collective-permute-start(f32[1,32,128]{2,1,0:T(8,128)S(1)} %get-tuple-element.15), channel_id=1, source_target_pairs={{0,1},{1,2},{2,3},{3,4},{4,5},{5,6},{6,7},{7,8},{8,9},{9,10},{10,1... | collective-permute-start | bytes 49160 | tf_op jit(solution)/shard_map/ppermute | solution.py:16
  438.2 5.1 copy-start.1
  443.3 709.3 %all-reduce.8.cloned.1.call-start = ((), (), s32[]{:S(2)}) async-start(), calls=%async_computation.2 | async-start | bytes 524288 | tf_op jit(solution)/shard_map/psum | solution.py:81
Sparse Core Ops, SparseCore 0:
  12.9 248.2 all-gather.2
  443.4 130.3 reduce-scatter.1
  576.7 575.8 all-reduce.7
where the time goes:
time: 1160 us
  waiting for transfers between devices  963 us (83%)
  blocking collectives  138 us (12%)
  starting transfers between devices  24.2 us (2%)
  between operations  16.6 us (1%)
    psum x1, waiting for transfers between devices, local(): moments = lax.psum(partial_rows, 'grp')  579 us
    all_gather x1, waiting for transfers between devices, local(): pieces = lax.all_gather(bundle[None], 'grp', axis=0, tiled=True)  248 us
    psum x1, blocking collectives, local(): weight_sum = lax.psum(jnp.sum(weights), 'grp')  138 us
    reduce_scatter x1, waiting for transfers between devices, local(): lax.psum_scatter(share * product, 'tile', scatter_dimension=0, tiled=True)  130 us
  transfers between devices with their start and end apart: 11, of which 6 were waited for; matrix products, arithmetic and copies ran while one was open for 0% of the time, Pallas kernels for 0%

commit v1 on v0

--- a/solution.py
+++ b/solution.py
@@ -48,10 +48,23 @@
 
 
 def local(log_cond, potential, noise, source, parents, accept, weights):
+
+    def fit_edges(d0, array_in):
+        kept_arr = jnp.concatenate(
+            lax.all_to_all(
+                jnp.stack(tuple((array_in for _ in range(lax.axis_size("grp"))))),
+                "grp",
+                split_axis=0,
+                concat_axis=0,
+            ),
+            d0,
+        )
+        return kept_arr
+
     mine = lax.axis_index("grp")
     bundle = jnp.stack([log_cond[0], potential[0]])
     parent = parents[mine]
-    pieces = lax.all_gather(bundle[None], "grp", axis=0, tiled=True)
+    pieces = fit_edges(0, bundle[None])
     owners = jnp.arange(pieces.shape[0], dtype=jnp.int32)
     chosen = jnp.where((owners == parent)[:, None, None, None, None], pieces, 0.0)
     moved = jnp.sum(chosen, axis=0)

time: 1160 us -> 1340 us (1.16)
  starting transfers between devices: 24.2 us -> 215 us
  waiting for transfers between devices: 963 us -> 942 us
    all_gather x1 -> x0, waiting for transfers between devices: 248 us -> none  [local(): pieces = lax.all_gather(bundle[None], 'grp', axis=0, tiled=True)]
    ppermute x4, starting transfers between devices: 18.9 us -> 189 us  [with_halo(): lax.ppermute(lax.slice_in_dim(block, block.shape[dim] - width, None, axis...]
    all_to_all x0 -> x1, waiting for transfers between devices: none -> 147 us  [fit_edges(): lax.all_to_all(jnp.stack(tuple((array_in for _ in range(lax.axis_size('gr...]
    ppermute x4, waiting for transfers between devices: 5.69 us -> 63.8 us  [with_halo(): lax.ppermute(lax.slice_in_dim(block, 0, width, axis=dim), axis, backward)]
    reduce_scatter x1, waiting for transfers between devices: 130 us -> 152 us  [local(): lax.psum_scatter(share * product, 'tile', scatter_dimension=0, tiled=True)]
    all_to_all x0 -> x1, starting transfers between devices: none -> 20.9 us  [fit_edges(): lax.all_to_all(jnp.stack(tuple((array_in for _ in range(lax.axis_size('gr...]
where the time goes in v1:
time: 1340 us
  waiting for transfers between devices  942 us (70%)
  starting transfers between devices  215 us (16%)
  blocking collectives  148 us (11%)
  between operations  16.9 us (1%)
    psum x1, waiting for transfers between devices, local(): moments = lax.psum(partial_rows, 'grp')  579 us
    ppermute x4, starting transfers between devices, with_halo(): lax.ppermute(lax.slice_in_dim(block, block.shape[dim] - width, None, axis...  189 us
    reduce_scatter x1, waiting for transfers between devices, local(): lax.psum_scatter(share * product, 'tile', scatter_dimension=0, tiled=True)  152 us
    psum x1, blocking collectives, local(): weight_sum = lax.psum(jnp.sum(weights), 'grp')  148 us
    all_to_all x1, waiting for transfers between devices, fit_edges(): lax.all_to_all(jnp.stack(tuple((array_in for _ in range(lax.axis_size('gr...  147 us
    ppermute x4, waiting for transfers between devices, with_halo(): lax.ppermute(lax.slice_in_dim(block, 0, width, axis=dim), axis, backward)  63.8 us
  transfers between devices with their start and end apart: 11, of which 6 were waited for; matrix products, arithmetic and copies ran while one was open for 0% of the time, Pallas kernels for 0%

profile of v1, /device:TPU:14, one launch (start us, length us, event | category | flops | bytes accessed | tf_op | source)
XLA Modules:
  0.0 1343.1 jit_solution(747564824424621438)
XLA Ops:
  7.2 1.0 pad_maximum_fusion.2
  8.2 4.3 stack.18
  12.5 0.0 copy-start.3
  12.5 0.0 copy-start.4
  12.5 20.9 %all-to-all-start = ((f32[32,1,2,8,32,128]{5,4,3,2,1,0:T(8,128)}), f32[32,1,2,8,32,128]{5,4,3,2,1,0:T(8,128)}, u32[]{:S(2)}, u32[]{:S(2)}) async-start(f32[32,1,2,8,32,128]{5,4,3,2,1,0:T(8,128)} %stack.18), calls=%async_computation | async-start | bytes 16777216 | tf_op jit(solution)/shard_map/all_to_all | solution.py:54
  33.4 0.0 copy-start.2
  33.4 0.0 copy-start
  33.5 0.0 reduce-scatter.2.cloned.1.call-start
  33.5 0.0 copy-done.3
  33.5 0.6 fusion.102
  35.4 0.0 copy-done.4
  35.4 0.6 dynamic_slice.3
  36.0 0.6 iota_compare_fusion.4
  36.7 146.8 %all-to-all-done = f32[32,1,2,8,32,128]{5,4,3,2,1,0:T(8,128)} async-done(((f32[32,1,2,8,32,128]{5,4,3,2,1,0:T(8,128)}), f32[32,1,2,8,32,128]{5,4,3,2,1,0:T(8,128)}, u32[]{:S(2)}, u32[]{:S(2)}) %all-to-all-start) | async-done | bytes 8388640 | tf_op jit(solution)/shard_map/all_to_all | solution.py:54
  183.5 4.6 fusion
  188.1 0.0 copy-done.2
  188.1 0.7 broadcast_select_fusion
  188.8 1.3 collective-permute-start
  190.1 1.3 collective-permute-start.1
  191.4 0.0 collective-permute-done
  191.4 31.6 %collective-permute-done.1 = f32[2,1,32,128]{3,2,1,0:T(8,128)S(1)} collective-permute-done((f32[2,1,32,128]{3,2,1,0:T(8,128)S(1)}, f32[2,1,32,128]{3,2,1,0:T(8,128)S(1)}, u32[]{:S(2)}, u32[]{:S(2)}) %collective-permute-start.1) | collective-permute-done | bytes 32800 | tf_op jit(solution)/shard_map/ppermute | solution.py:19
  223.1 0.0 copy-done
  223.1 0.3 fusion.12
  223.4 1.3 collective-permute-start.2
  224.7 68.3 %collective-permute-start.3 = (f32[1,32,128]{2,1,0:T(8,128)S(1)}, f32[1,32,128]{2,1,0:T(8,128)S(1)}, u32[]{:S(2)}, u32[]{:S(2)}) collective-permute-start(f32[1,32,128]{2,1,0:T(8,128)S(1)} %get-tuple-element.17), channel_id=1, source_target_pairs={{0,1},{1,2},{2,3},{3,4},{4,5},{5,6},{6,7},{7,8},{8,9},{9,10},{10,1... | collective-permute-start | bytes 49160 | tf_op jit(solution)/shard_map/ppermute | solution.py:16
  293.0 0.0 collective-permute-done.2
  293.0 0.8 collective-permute-done.3
  293.8 0.2 select_maximum_fusion.2
  294.0 0.3 fusion.86
  294.3 13.7 %collective-permute-start.4 = (f32[2,1,32,128]{3,2,1,0:T(8,128)S(1)}, f32[2,1,32,128]{3,2,1,0:T(8,128)S(1)}, u32[]{:S(2)}, u32[]{:S(2)}) collective-permute-start(f32[2,1,32,128]{3,2,1,0:T(8,128)S(1)} %get-tuple-element.10), channel_id=1, source_target_pairs={{0,1},{1,2},{2,3},{3,4},{4,5},{5,6},{6,7},{7,8},{8,9},{9,10},{10,1... | collective-permute-start | bytes 98312 | tf_op jit(solution)/shard_map/ppermute | solution.py:16
  308.0 1.3 collective-permute-start.5
  309.3 0.0 collective-permute-done.4
  309.3 32.2 %collective-permute-done.5 = f32[2,1,32,128]{3,2,1,0:T(8,128)S(1)} collective-permute-done((f32[2,1,32,128]{3,2,1,0:T(8,128)S(1)}, f32[2,1,32,128]{3,2,1,0:T(8,128)S(1)}, u32[]{:S(2)}, u32[]{:S(2)}) %collective-permute-start.5) | collective-permute-done | bytes 32800 | tf_op jit(solution)/shard_map/ppermute | solution.py:19
  341.6 0.3 fusion.24
  341.9 1.3 collective-permute-start.6
  343.2 105.9 %collective-permute-start.7 = (f32[1,32,128]{2,1,0:T(8,128)S(1)}, f32[1,32,128]{2,1,0:T(8,128)S(1)}, u32[]{:S(2)}, u32[]{:S(2)}) collective-permute-start(f32[1,32,128]{2,1,0:T(8,128)S(1)} %get-tuple-element.15), channel_id=1, source_target_pairs={{0,1},{1,2},{2,3},{3,4},{4,5},{5,6},{6,7},{7,8},{8,9},{9,10},{10,1... | collective-permute-start | bytes 49160 | tf_op jit(solution)/shard_map/ppermute | solution.py:16
  449.1 147.6 %psum.14 = f32[]{:T(128)} all-reduce(f32[]{:T(128)} %bitcast.17), channel_id=1, replica_groups=mesh['grp'=32,'tile'=16] {'grp'}, use_global_device_ids=true, to_apply=%region_1.2 | all-reduce | flops 1 | bytes 8 | tf_op jit(solution)/shard_map/psum | solution.py:83
  597.9 0.0 collective-permute-done.6
  597.9 0.0 collective-permute-done.7
  597.9 0.2 select_maximum_fusion
  598.1 0.3 fusion.67
  598.4 0.0 copy-start.1
  598.4 5.1 convolution_multiply_fusion
  603.6 0.0 reduce-scatter.2.cloned.1.call-update
  603.6 0.0 all-reduce.8.cloned.1.call-start
  603.6 152.2 %reduce-scatter.2.cloned.1.call-done = f32[64,1024]{1,0:T(8,128)} async-done(((f32[1024,1024]{1,0:T(8,128)}), f32[64,1024]{1,0:T(8,128)}) %reduce-scatter.2.cloned.1.call-update) | async-done | bytes 262160 | tf_op jit(solution)/shard_map/reduce_scatter | solution.py:93
  755.9 0.0 all-reduce.8.cloned.1.call-update
  755.9 578.8 %all-reduce.8.cloned.1.call-done = f32[64,1024]{1,0:T(8,128)} async-done(((f32[64,1024]{1,0:T(8,128)}), f32[64,1024]{1,0:T(8,128)}) %all-reduce.8.cloned.1.call-update) | async-done | bytes 262160 | tf_op jit(solution)/shard_map/psum | solution.py:94
  1334.6 1.7 copy.19
  1336.3 0.0 copy-done.1
  (8 shorter events, 0.1 us)
Async XLA Ops:
  12.5 21.0 %copy-start.3 = (s32[2,1]{0,1:T(1,128)S(1)}, s32[2,1]{0,1:T(1,128)}, u32[]{:S(2)}) copy-start(s32[2,1]{0,1:T(1,128)} %param.12) | copy-start | bytes 28
  12.5 22.9 %copy-start.4 = (s32[32]{0:T(128)S(1)}, s32[32]{0:T(128)}, u32[]{:S(2)}) copy-start(s32[32]{0:T(128)} %param.11) | copy-start | bytes 388
  12.5 171.0 %all-to-all-start = ((f32[32,1,2,8,32,128]{5,4,3,2,1,0:T(8,128)}), f32[32,1,2,8,32,128]{5,4,3,2,1,0:T(8,128)}, u32[]{:S(2)}, u32[]{:S(2)}) async-start(f32[32,1,2,8,32,128]{5,4,3,2,1,0:T(8,128)} %stack.18), calls=%async_computation | async-start | bytes 16777216 | tf_op jit(solution)/shard_map/all_to_all | solution.py:54
  33.4 154.6 %copy-start.2 = (f32[2,1,8,32,128]{4,3,2,1,0:T(8,128)S(1)}, f32[2,1,8,32,128]{4,3,2,1,0:T(8,128)}, u32[]{:S(2)}) copy-start(f32[2,1,8,32,128]{4,3,2,1,0:T(8,128)} %param.9) | copy-start | bytes 786436
  33.4 189.7 %copy-start = (f32[8,32,128]{2,1,0:T(8,128)S(1)}, f32[8,32,128]{2,1,0:T(8,128)}, u32[]{:S(2)}) copy-start(f32[8,32,128]{2,1,0:T(8,128)} %param.10) | copy-start | bytes 393220
  33.5 722.4 %reduce-scatter.2.cloned.1.call-start = ((), (), s32[]{:S(2)}) async-start(), calls=%async_computation.2 | async-start | bytes 4456448 | tf_op jit(solution)/shard_map/reduce_scatter | solution.py:93
  188.8 2.6 collective-permute-start
  190.1 33.0 %collective-permute-start.1 = (f32[2,1,32,128]{3,2,1,0:T(8,128)S(1)}, f32[2,1,32,128]{3,2,1,0:T(8,128)S(1)}, u32[]{:S(2)}, u32[]{:S(2)}) collective-permute-start(f32[2,1,32,128]{3,2,1,0:T(8,128)S(1)} %get-tuple-element.13), channel_id=1, source_target_pairs={{1,0},{2,1},{3,2},{4,3},{5,4},{6,5},{7,6},{8,7},{9,8},{10,9},{11,1... | collective-permute-start | bytes 98312 | tf_op jit(solution)/shard_map/ppermute | solution.py:19
  223.4 69.6 %collective-permute-start.2 = (f32[1,32,128]{2,1,0:T(8,128)S(1)}, f32[1,32,128]{2,1,0:T(8,128)S(1)}, u32[]{:S(2)}, u32[]{:S(2)}) collective-permute-start(f32[1,32,128]{2,1,0:T(8,128)S(1)} %get-tuple-element.18), channel_id=1, source_target_pairs={{1,0},{2,1},{3,2},{4,3},{5,4},{6,5},{7,6},{8,7},{9,8},{10,9},{11,1... | collective-permute-start | bytes 49160 | tf_op jit(solution)/shard_map/ppermute | solution.py:19
  224.7 69.1 %collective-permute-start.3 = (f32[1,32,128]{2,1,0:T(8,128)S(1)}, f32[1,32,128]{2,1,0:T(8,128)S(1)}, u32[]{:S(2)}, u32[]{:S(2)}) collective-permute-start(f32[1,32,128]{2,1,0:T(8,128)S(1)} %get-tuple-element.17), channel_id=1, source_target_pairs={{0,1},{1,2},{2,3},{3,4},{4,5},{5,6},{6,7},{7,8},{8,9},{9,10},{10,1... | collective-permute-start | bytes 49160 | tf_op jit(solution)/shard_map/ppermute | solution.py:16
  294.3 15.0 %collective-permute-start.4 = (f32[2,1,32,128]{3,2,1,0:T(8,128)S(1)}, f32[2,1,32,128]{3,2,1,0:T(8,128)S(1)}, u32[]{:S(2)}, u32[]{:S(2)}) collective-permute-start(f32[2,1,32,128]{3,2,1,0:T(8,128)S(1)} %get-tuple-element.10), channel_id=1, source_target_pairs={{0,1},{1,2},{2,3},{3,4},{4,5},{5,6},{6,7},{7,8},{8,9},{9,10},{10,1... | collective-permute-start | bytes 98312 | tf_op jit(solution)/shard_map/ppermute | solution.py:16
  308.0 33.5 %collective-permute-start.5 = (f32[2,1,32,128]{3,2,1,0:T(8,128)S(1)}, f32[2,1,32,128]{3,2,1,0:T(8,128)S(1)}, u32[]{:S(2)}, u32[]{:S(2)}) collective-permute-start(f32[2,1,32,128]{3,2,1,0:T(8,128)S(1)} %get-tuple-element.11), channel_id=1, source_target_pairs={{1,0},{2,1},{3,2},{4,3},{5,4},{6,5},{7,6},{8,7},{9,8},{10,9},{11,1... | collective-permute-start | bytes 98312 | tf_op jit(solution)/shard_map/ppermute | solution.py:19
  341.9 256.1 %collective-permute-start.6 = (f32[1,32,128]{2,1,0:T(8,128)S(1)}, f32[1,32,128]{2,1,0:T(8,128)S(1)}, u32[]{:S(2)}, u32[]{:S(2)}) collective-permute-start(f32[1,32,128]{2,1,0:T(8,128)S(1)} %get-tuple-element.16), channel_id=1, source_target_pairs={{1,0},{2,1},{3,2},{4,3},{5,4},{6,5},{7,6},{8,7},{9,8},{10,9},{11,1... | collective-permute-start | bytes 49160 | tf_op jit(solution)/shard_map/ppermute | solution.py:19
  343.2 254.8 %collective-permute-start.7 = (f32[1,32,128]{2,1,0:T(8,128)S(1)}, f32[1,32,128]{2,1,0:T(8,128)S(1)}, u32[]{:S(2)}, u32[]{:S(2)}) collective-permute-start(f32[1,32,128]{2,1,0:T(8,128)S(1)} %get-tuple-element.15), channel_id=1, source_target_pairs={{0,1},{1,2},{2,3},{3,4},{4,5},{5,6},{6,7},{7,8},{8,9},{9,10},{10,1... | collective-permute-start | bytes 49160 | tf_op jit(solution)/shard_map/ppermute | solution.py:16
  598.4 737.9 %copy-start.1 = (f32[8,32,128]{2,1,0:T(8,128)}, f32[8,32,128]{2,1,0:T(8,128)S(1)}, u32[]{:S(2)}) copy-start(f32[8,32,128]{2,1,0:T(8,128)S(1)} %fusion.67) | copy-start | bytes 393220
  603.6 731.1 %all-reduce.8.cloned.1.call-start = ((), (), s32[]{:S(2)}) async-start(), calls=%async_computation.3 | async-start | bytes 524288 | tf_op jit(solution)/shard_map/psum | solution.py:94
Sparse Core Ops, SparseCore 0:
  603.7 152.1 reduce-scatter.1
  758.8 575.8 all-reduce.7
